TPU v7x, 32 devices: a whole 2x2x4 slice. The times are simulated.
32 devices in a mesh: pipe: 4 (over x, core), sp: 2 (over y), dp: 4 (over z).
Axes of the slice: x: 2, y: 2, z: 4, core: 2. Of those that a mesh axis runs over, the one named last changes fastest.
Arguments:
- fresh_input: bfloat16 [4, 4, 120, 240, 128], P('pipe', 'dp', 'sp'), may hold values from -6 to 6
- saved_input: bfloat16 [4, 4, 120, 240, 128], P('pipe', 'dp', 'sp'), may hold values from -6 to 6
- output_grad: bfloat16 [4, 4, 120, 240, 128], P('pipe', 'dp', 'sp'), may hold values from -6 to 6
- expand_weight: bfloat16 [4, 128, 768], P('pipe'), may hold values from -0.5 to 0.5
- reduce_weight: bfloat16 [4, 768, 128], P('pipe'), may hold values from -0.21875 to 0.21875
- filter_weight: float32 [4, 2, 120, 128], P('pipe'), may hold values from -6 to 6
- cycle_table: int32 [120], replicated, may hold values from 0 to 119, each once
Outputs:
- next_input: bfloat16 [4, 4, 120, 240, 128], P('pipe', 'dp', 'sp')
- input_grad: bfloat16 [4, 4, 120, 240, 128], P('pipe', 'dp', 'sp')
- expand_grad: float32 [4, 128, 768], P('pipe', None, 'dp')
- reduce_grad: float32 [4, 768, 128], P('pipe', 'dp')
- filter_grad: float32 [4, 2, 120, 128], P('pipe')
Inputs may be any that keep to these rules, and one draw needn't show every extreme that they name: `cycle_table`: each of 0 .. 119 appears once; values 120 or more mark empty cycle slots.
All inputs are finite; a program needn't handle non-finite values.
Results may differ from a plain program's by a relative error of at most 0.025.
Values may be sent and summed in bfloat16 or wider, within the bound.
A program may use at most 192 MiB of HBM per device.

v0:
```python
import math
import jax
import jax.numpy as jnp
from jax import lax
from jax.sharding import PartitionSpec as P

NLAT = 120
NLON = 240
ROOT_HALF = 0.7071067811865476
INV_ROOT_TAU = 0.3989422804014327


def from_behind(block, axis, distance):
    devices = range(lax.axis_size(axis))
    route = [(i - distance, i) for i in devices if i - distance in devices]
    return lax.ppermute(block, axis, route)


def gelu_value(pre_act):
    return 0.5 * pre_act * (1.0 + lax.erf(pre_act * ROOT_HALF))


def gelu_slope(pre_act):
    return (
        0.5 * (1.0 + lax.erf(pre_act * ROOT_HALF))
        + pre_act * jnp.exp(-0.5 * pre_act * pre_act) * INV_ROOT_TAU
    )


def legendre(lat_index, order_index, cycles):
    lat_ok = (lat_index < cycles).astype(jnp.float32)
    order_ok = (order_index < cycles).astype(jnp.float32)
    colatitude = math.pi * (jnp.minimum(lat_index, cycles - 1).astype(jnp.float32) + 0.5) / cycles
    cosine = jnp.cos(colatitude)[None, :]
    sine_value = jnp.sin(colatitude)[None, :]
    order_value = jnp.minimum(order_index, cycles - 1).astype(jnp.float32)[:, None]
    log_start = 0.5 * (
        jnp.log((2.0 * order_value + 1.0) / (4.0 * math.pi))
        + lax.lgamma(2.0 * order_value + 1.0)
        - 2.0 * lax.lgamma(order_value + 1.0)
        - order_value * math.log(4.0)
    ) + order_value * jnp.log(sine_value)
    starting = jnp.exp(log_start)
    zero_rows = jnp.zeros_like(starting)

    def advance(state_pair, degree):
        previous, earlier = state_pair
        degree_value = degree.astype(jnp.float32)
        upper_term = jnp.maximum(4.0 * degree_value * degree_value - 1.0, 0.0)
        ratio_main = jnp.sqrt(
            upper_term / jnp.maximum(degree_value * degree_value - order_value * order_value, 1.0)
        )
        ratio_back = jnp.sqrt(
            jnp.maximum((degree_value - 1.0) ** 2 - order_value * order_value, 0.0)
            / jnp.maximum(4.0 * (degree_value - 1.0) ** 2 - 1.0, 1.0)
        )
        rising = ratio_main * (cosine * previous - ratio_back * earlier)
        current = jnp.where(
            degree_value == order_value,
            starting,
            jnp.where(degree_value > order_value, rising, 0.0),
        )
        return ((current, previous), current)

    _, stacked = lax.scan(advance, (zero_rows, zero_rows), jnp.arange(cycles, dtype=jnp.int32))
    valid_mask = order_ok[:, None] * lat_ok[None, :]
    return jnp.transpose(stacked, (1, 0, 2)) * valid_mask[:, None, :]


def cycle_weights(lat_index, cycles):
    valid_cycle = (lat_index < cycles).astype(jnp.float32)
    colatitude = math.pi * (jnp.minimum(lat_index, cycles - 1).astype(jnp.float32) + 0.5) / cycles
    return math.pi / cycles * jnp.sin(colatitude) * valid_cycle


def fourier_tables(order_index, cycles, points):
    valid_order = (order_index < cycles).astype(jnp.float32)[None, :]
    order_value = jnp.minimum(order_index, cycles - 1)
    longitude = jnp.arange(points, dtype=jnp.int32)
    phase_angle = (
        2.0
        * math.pi
        / points
        * (longitude[:, None] * order_value[None, :] % points).astype(jnp.float32)
    )
    scaled = valid_order * (2.0 * math.pi / points)
    forward = jnp.concatenate(
        [jnp.cos(phase_angle) * scaled, -jnp.sin(phase_angle) * scaled], axis=1
    )
    order_scale = jnp.where(order_value == 0, 1.0, 2.0)[None, :] * valid_order / (2.0 * math.pi)
    inverse = jnp.concatenate(
        [jnp.cos(phase_angle) * order_scale, -jnp.sin(phase_angle) * order_scale], axis=1
    ).T
    return (forward.astype(jnp.bfloat16), inverse.astype(jnp.bfloat16))


def joint_orders(coeffs):
    return lax.all_to_all(coeffs, "sp", split_axis=3, concat_axis=1, tiled=True)


def joint_cycles(values):
    return lax.all_to_all(values, "sp", split_axis=1, concat_axis=3, tiled=True)


def spectral_pass(tokens, filt, forward, analysis, synthesis, inverse, to_orders, to_cycles):
    batch_count, row_count, points, chan_count = tokens.shape
    order_count = forward.shape[1] // 2
    coeffs = jnp.einsum(
        "sjnc,nk->sjkc", tokens, forward, preferred_element_type=jnp.float32
    ).astype(jnp.bfloat16)
    coeffs = coeffs.reshape(batch_count, row_count, 2, order_count, chan_count)
    arrived = to_orders(coeffs)
    spectra = jnp.einsum("tlj,sjrtc->strlc", analysis, arrived, preferred_element_type=jnp.float32)
    real_part = filt[0] * spectra[:, :, 0] - filt[1] * spectra[:, :, 1]
    imag_part = filt[0] * spectra[:, :, 1] + filt[1] * spectra[:, :, 0]
    filtered = jnp.stack([real_part, imag_part], axis=2).astype(jnp.bfloat16)
    values = jnp.einsum(
        "tlj,strlc->sjrtc", synthesis, filtered, preferred_element_type=jnp.float32
    ).astype(jnp.bfloat16)
    returned = to_cycles(values).reshape(batch_count, row_count, 2 * order_count, chan_count)
    spatial = jnp.einsum("sjkc,kn->sjnc", returned, inverse, preferred_element_type=jnp.float32)
    return (spatial, spectra)


def mlp_pass(tokens, spatial, expand, contract, cycle_mask):
    grid_shape = tokens.shape
    flat_rows = (tokens.astype(jnp.float32) + spatial).reshape(-1, grid_shape[-1])
    mixed_b = flat_rows.astype(jnp.bfloat16)
    hidden_pre = jnp.dot(mixed_b, expand, preferred_element_type=jnp.float32)
    hidden = gelu_value(hidden_pre).astype(jnp.bfloat16)
    result = flat_rows + jnp.dot(hidden, contract, preferred_element_type=jnp.float32)
    result = (result.reshape(grid_shape) * cycle_mask[:, None, None]).astype(jnp.bfloat16)
    return (result, mixed_b, hidden_pre, hidden)


def backward_rows(cotangent, cycle_mask, mixed_b, hidden_pre, hidden, expand, contract):
    chan_count = cotangent.shape[-1]
    masked = (cotangent * cycle_mask.astype(jnp.bfloat16)[:, None, None]).reshape(-1, chan_count)
    grad_reduce = jnp.dot(hidden.T, masked, preferred_element_type=jnp.float32)
    grad_hidden = jnp.dot(masked, contract.T, preferred_element_type=jnp.float32)
    grad_pre = (grad_hidden * gelu_slope(hidden_pre)).astype(jnp.bfloat16)
    grad_expand = jnp.dot(mixed_b.T, grad_pre, preferred_element_type=jnp.float32)
    grad_mixed = masked.astype(jnp.float32) + jnp.dot(
        grad_pre, expand.T, preferred_element_type=jnp.float32
    )
    return (grad_mixed, grad_expand, grad_reduce)


def on_device(
    fresh_input, saved_input, output_grad, expand_weight, reduce_weight, filter_weight, cycle_table
):
    slot_count = fresh_input.shape[2]
    position = lax.axis_index("sp")
    order_table = jnp.arange(slot_count * lax.axis_size("sp"), dtype=jnp.int32)
    own_cycles = lax.dynamic_slice_in_dim(cycle_table, position * slot_count, slot_count)
    own_orders = lax.dynamic_slice_in_dim(order_table, position * slot_count, slot_count)
    cycle_mask = (own_cycles < NLAT).astype(jnp.float32)
    table = legendre(cycle_table, own_orders, NLAT)
    analysis = (table * cycle_weights(cycle_table, NLAT)[None, None, :]).astype(jnp.bfloat16)
    synthesis = table.astype(jnp.bfloat16)
    forward, inverse = fourier_tables(order_table, NLAT, NLON)
    filt = filter_weight[0]
    expand = expand_weight[0]
    contract = reduce_weight[0]
    fresh = fresh_input[0, 0]
    saved = saved_input[0, 0]
    spatial, spectra = spectral_pass(
        jnp.stack([fresh, saved]),
        filt,
        forward,
        analysis,
        synthesis,
        inverse,
        joint_orders,
        joint_cycles,
    )
    fresh_spatial = spatial[0]
    saved_spatial = spatial[1]
    saved_spectra = spectra[1]
    block = mlp_pass(fresh, fresh_spatial, expand, contract, cycle_mask)[0]
    next_input = from_behind(block[None, None], "pipe", 1)
    _, mixed_b, hidden_pre, hidden = mlp_pass(saved, saved_spatial, expand, contract, cycle_mask)
    grad_mixed, grad_expand, grad_reduce = backward_rows(
        output_grad[0, 0], cycle_mask, mixed_b, hidden_pre, hidden, expand, contract
    )
    grid_shape = saved.shape
    row_count, points, chan_count = grid_shape
    order_count = forward.shape[1] // 2
    grad_rows = grad_mixed.reshape(grid_shape).astype(jnp.bfloat16)
    grad_values = jnp.einsum(
        "jnc,kn->jkc", grad_rows, inverse, preferred_element_type=jnp.float32
    ).astype(jnp.bfloat16)
    grad_values = grad_values.reshape(row_count, 2, order_count, chan_count)
    arrived = lax.all_to_all(grad_values, "sp", split_axis=2, concat_axis=0, tiled=True)
    grad_filtered = jnp.einsum(
        "tlj,jrtc->trlc", synthesis, arrived, preferred_element_type=jnp.float32
    )
    filter_real = jnp.sum(
        grad_filtered[:, 0] * saved_spectra[:, 0] + grad_filtered[:, 1] * saved_spectra[:, 1],
        axis=0,
    )
    filter_imag = jnp.sum(
        grad_filtered[:, 1] * saved_spectra[:, 0] - grad_filtered[:, 0] * saved_spectra[:, 1],
        axis=0,
    )
    grad_spectra = jnp.stack(
        [
            filt[0] * grad_filtered[:, 0] + filt[1] * grad_filtered[:, 1],
            filt[0] * grad_filtered[:, 1] - filt[1] * grad_filtered[:, 0],
        ],
        axis=1,
    ).astype(jnp.bfloat16)
    grad_coeffs = jnp.einsum(
        "tlj,trlc->jrtc", analysis, grad_spectra, preferred_element_type=jnp.float32
    ).astype(jnp.bfloat16)
    returned = lax.all_to_all(grad_coeffs, "sp", split_axis=0, concat_axis=2, tiled=True)
    grad_tokens = jnp.einsum(
        "jkc,nk->jnc",
        returned.reshape(row_count, 2 * order_count, chan_count),
        forward,
        preferred_element_type=jnp.float32,
    )
    input_grad = (
        (grad_mixed.reshape(grid_shape) + grad_tokens) * cycle_mask[:, None, None]
    ).astype(jnp.bfloat16)
    sent_back = from_behind(input_grad[None, None], "pipe", -1)
    filter_grad = lax.psum(jnp.stack([filter_real, filter_imag]), ("sp", "dp"))
    summed = (
        lax.psum(grad_expand.astype(jnp.bfloat16), "sp").astype(jnp.float32),
        lax.psum(grad_reduce.astype(jnp.bfloat16), "sp").astype(jnp.float32),
    )
    expand_grad, reduce_grad = (
        lax.psum_scatter(
            summed[0].astype(jnp.bfloat16), "dp", scatter_dimension=1, tiled=True
        ).astype(jnp.float32),
        lax.psum_scatter(
            summed[1].astype(jnp.bfloat16), "dp", scatter_dimension=0, tiled=True
        ).astype(jnp.float32),
    )
    return (next_input, sent_back, expand_grad[None], reduce_grad[None], filter_grad[None])


def solution(mesh):
    return jax.shard_map(
        on_device,
        mesh=mesh,
        in_specs=(
            P("pipe", "dp", "sp", None, None),
            P("pipe", "dp", "sp", None, None),
            P("pipe", "dp", "sp", None, None),
            P("pipe", None, None),
            P("pipe", None, None),
            P("pipe", None, None, None),
            P(),
        ),
        out_specs=(
            P("pipe", "dp", "sp", None, None),
            P("pipe", "dp", "sp", None, None),
            P("pipe", None, "dp"),
            P("pipe", "dp", None),
            P("pipe", None, None, None),
        ),
        check_vma=False,
    )
```

profile of v0, /device:TPU:0, one launch (start us, length us, event | category | flops | bytes accessed | tf_op | source)
XLA Modules:
  0.0 807.0 jit_solution(4464652124420981998)
XLA Ops:
  8.7 5.3 fusion.33
  14.0 8.9 %copy.39 = bf16[2,60,2,120,128]{4,2,1,0,3:T(2,128)(2,1)} copy(bf16[2,60,2,120,128]{4,3,2,1,0:T(8,128)(2,1)S(1)} %bitcast.168) | data formatting | bytes 14745600 | tf_op jit(solution)/shard_map/reshape | solution.py:111
  22.9 6.9 all-to-all-start
  30.1 240.9 %while.18 = (s32[]{:T(128)}, f32[60,120]{1,0:T(8,128)S(1)}, f32[60,120]{1,0:T(8,128)S(1)}, f32[120,60,120]{2,1,0:T(8,128)}, s32[120]{0:T(128)S(1)}, /*index=5*/f...) while((s32[]{:T(128)}, f32[60,120]{1,0:T(8,128)S(1)}, ...), condition=%wide.region_1.2_spmd.clone, body=%wide.region_0.1_spmd.clone.sunk | while | flops 65294 | bytes 151427 | solution.py:65
  271.9 4.3 broadcast_multiply_fusion
  276.2 3.9 fusion.61
  280.1 7.4 copy.41
  287.5 12.1 %convolution_bitcast_fusion = f32[2,60,2,120,128]{4,3,2,0,1:T(8,128)} fusion(bf16[2,120,2,60,128]{4,2,3,1,0:T(2,128)(2,1)} %bitcast.162, bf16[60,120,120,1,1]{2,0,1,4,3:T(8,128)(2,1)S(1)} %get-tuple-element.230), kind=kOutput, calls=%fused_computation.24 | convolution fusion | flops 884736000 | bytes 23846400 | tf_op jit(solution)/shard_map/tlj,sjrtc->strlc/dot_general | solution.py:113
  299.6 8.6 %subtract_convert_fusion = (bf16[2,60,1,120,128]{4,3,2,0,1:T(8,128)(2,1)}, bf16[2,60,1,120,128]{4,3,2,0,1:T(8,128)(2,1)}) fusion(f32[2,60,2,120,128]{4,3,2,0,1:T(8,128)} %convolution_bitcast_fusion, f32[120,128]{1,0:T(8,128)S(1)} %get-tuple-element.234, f32[120,128]{1,0:T(8,128)S(1)} %get-tuple-element.233), kind=kLoop, calls=%fused_computation.48 | loop fusion | flops 14745600 | bytes 22241280 | tf_op jit(solution)/shard_map/convert.6
  308.2 11.1 %convert_bitcast_fusion = bf16[2,120,2,60,128]{4,1,2,0,3:T(8,128)(2,1)} fusion(bf16[2,60,1,120,128]{4,3,2,0,1:T(8,128)(2,1)} %get-tuple-element.220, bf16[2,60,1,120,128]{4,3,2,0,1:T(8,128)(2,1)} %get-tuple-element.219, bf16[60,120,120,1,1]{2,0,1,4,3:T(8,128)(2,1)S(1)} %copy-done.7), kind=kOutput, calls=%fused_computation.46 | convolution fusion | flops 892108800 | bytes 16473600 | tf_op jit(solution)/shard_map/tlj,strlc->sjrtc/dot_general | solution.py:117
  319.2 11.9 %copy.45 = bf16[2,120,2,60,128]{4,2,0,3,1:T(2,128)(2,1)} copy(bf16[2,120,2,60,128]{4,1,2,0,3:T(8,128)(2,1)} %convert_bitcast_fusion) | data formatting | bytes 14745600 | tf_op jit(solution)/shard_map/convert_element_type | solution.py:119
  331.1 6.7 all-to-all-start.1
  337.8 9.4 %bitcast_multiply_fusion = bf16[14400,128]{1,0:T(8,128)(2,1)} fusion(bf16[1,1,60,240,128]{4,3,2,1,0:T(8,128)(2,1)} %param.11, bf16[14400]{0:T(1024)(128)(2,1)S(1)} %mul.489), kind=kLoop, calls=%fused_computation.58 | loop fusion | flops 1843200 | bytes 7401600 | tf_op jit(solution)/shard_map/mul | solution.py:138
  347.2 6.6 slice_bitcast_fusion
  353.8 67.0 %all-to-all-done.1 = bf16[2,120,2,60,128]{4,2,0,3,1:T(2,128)(2,1)} async-done(((bf16[2,120,2,60,128]{4,2,0,3,1:T(2,128)(2,1)}), bf16[2,120,2,60,128]{4,2,0,3,1:T(2,128)(2,1)}, u32[]{:S(2)}, u32[]{:S(2)}) %all-to-all-start.1) | async-done | bytes 7372832 | tf_op jit(solution)/shard_map/all_to_all | solution.py:102
  420.9 11.0 %copy.47 = bf16[2,60,2,2,60,128]{5,0,4,3,2,1:T(2,128)(2,1)S(1)} copy(bf16[2,60,2,2,60,128]{5,2,0,4,1,3:T(2,128)(2,1)} %bitcast.25) | data formatting | bytes 14745600 | tf_op jit(solution)/shard_map/all_to_all | solution.py:102
  431.9 7.3 fusion.30
  439.2 12.9 %fusion.100 = (f32[1,60,240,128]{3,2,1,0:T(8,128)S(1)}, bf16[1,60,240,128]{3,2,1,0:T(8,128)(2,1)}, bf16[1,60,240,128]{3,2,1,0:T(8,128)(2,1)S(1)}, f32[1,60,240,128]{3,2,1,0:T(8,128)}) fusion(f32[2,60,240,128]{3,2,1,0:T(8,128)} %fusion.30, bf16[1,1,60,240,128]{4,3,2,1,0:T(8,128)(2,1)} %param.9, bf16[1,1,60,240,128]{4,3,2,1,0:T(8,128)(2,1)} %param.10), kind=kLoop, calls=%fused_computation.174 | loop fusion | flops 11059200 | bytes 44236800 | tf_op jit(solution)/shard_map/slice | solution.py:178
  452.1 3.7 fusion.22
  455.8 17.0 %fusion.65 = f32[14400,768]{1,0:T(8,128)} fusion(bf16[14400,128]{1,0:T(8,128)(2,1)S(1)} %bitcast.163, bf16[1,128,768]{2,1,0:T(8,128)(2,1)S(1)} %copy-done), kind=kOutput, calls=%fused_computation.84 | convolution fusion | flops 2831155200 | bytes 48119808 | tf_op jit(solution)/shard_map/dot_general | solution.py:129
  472.9 30.9 %fusion.7 = bf16[14400,768]{1,0:T(8,128)(2,1)} fusion(f32[14400,768]{1,0:T(8,128)} %fusion.65, bf16[14400,128]{1,0:T(8,128)(2,1)} %bitcast.170, bf16[1,768,128]{2,1,0:T(8,128)(2,1)S(1)} %copy-done.20), kind=kOutput, calls=%fused_computation.14 | convolution fusion | flops 2941747200 | bytes 70238208 | tf_op jit(solution)/shard_map/dot_general | solution.py:140
  503.8 10.9 %convolution_add_fusion = f32[14400,128]{1,0:T(8,128)S(1)} fusion(bf16[14400,768]{1,0:T(8,128)(2,1)} %fusion.7, bf16[14400,128]{1,0:T(8,128)(2,1)S(1)} %copy-done.2, bf16[1,128,768]{2,1,0:T(8,128)(2,1)S(1)} %copy-done), kind=kOutput, calls=%fused_computation.22 | convolution fusion | flops 2834841600 | bytes 33374208 | tf_op jit(solution)/shard_map/dot_general | solution.py:143
  515.9 1.8 copy-done.1
  517.7 4.6 copy.50
  522.4 5.4 all-to-all-start.2
  527.8 16.7 %fusion.11 = f32[14400,128]{1,0:T(8,128)} fusion(bf16[14400,128]{1,0:T(8,128)(2,1)} %bitcast.173, f32[14400,128]{1,0:T(8,128)} %bitcast.167, bf16[14400,128]{1,0:T(8,128)(2,1)} %bitcast.172, bf16[1,768,128]{2,1,0:T(8,128)(2,1)S(1)} %copy-done.20, bf16[1,128,768]{2,1,0:T(8,128)(2,1)S(1)} %copy-done), kind=kOutput, calls=%fused_computation.21 | convolution fusion | flops 5723136000 | bytes 22511616 | tf_op jit(solution)/shard_map/dot_general | solution.py:131
  544.5 5.6 multiply_convert_fusion.6
  550.1 3.3 collective-permute-start
  553.3 16.1 %all-to-all-done.2 = bf16[60,2,120,128]{3,1,0,2:T(2,128)(2,1)} async-done(((bf16[60,2,120,128]{3,1,0,2:T(2,128)(2,1)}), bf16[60,2,120,128]{3,1,0,2:T(2,128)(2,1)}, u32[]{:S(2)}, u32[]{:S(2)}) %all-to-all-start.2) | async-done | bytes 3686432 | tf_op jit(solution)/shard_map/all_to_all | solution.py:194
  569.5 4.7 copy.52
  574.2 1.9 fusion.45
  576.4 2.3 add_reduce_fusion
  578.7 4.8 convert_bitcast_fusion.1
  583.5 4.8 copy.56
  588.3 5.4 all-to-all-start.3
  593.8 14.8 %convolution_convert_fusion = bf16[128,768]{0,1:T(8,128)(2,1)} fusion(bf16[14400,128]{1,0:T(8,128)(2,1)} %fusion.22, bf16[14400,768]{1,0:T(8,128)(2,1)} %fusion.7), kind=kOutput, calls=%fused_computation.76 | convolution fusion | flops 2831253504 | bytes 26001408 | tf_op jit(solution)/shard_map/dot_general | solution.py:142
  608.6 25.9 %all-to-all-done.3 = bf16[120,2,60,128]{3,1,2,0:T(2,128)(2,1)} async-done(((bf16[120,2,60,128]{3,1,2,0:T(2,128)(2,1)}), bf16[120,2,60,128]{3,1,2,0:T(2,128)(2,1)}, u32[]{:S(2)}, u32[]{:S(2)}) %all-to-all-start.3) | async-done | bytes 3686432 | tf_op jit(solution)/shard_map/all_to_all | solution.py:216
  634.5 5.1 copy.57
  639.6 6.6 reshape.336
  646.2 7.4 fusion.36
  654.9 20.0 %fusion.57 = bf16[768,128]{1,0:T(8,128)(2,1)} fusion(bf16[14400,128]{1,0:T(8,128)(2,1)S(1)} %copy-done.3, f32[14400,768]{1,0:T(8,128)} %fusion.65), kind=kOutput, calls=%fused_computation.75 | convolution fusion | flops 2886549504 | bytes 48119808 | tf_op jit(solution)/shard_map/dot_general | solution.py:139
  675.0 22.3 %reduce-scatter.5.cloned.1.call-done = bf16[192,128]{1,0:T(8,128)(2,1)} async-done(((bf16[768,128]{1,0:T(8,128)(2,1)}), bf16[192,128]{1,0:T(8,128)(2,1)}) %reduce-scatter.5.cloned.1.call-update) | async-done | bytes 49168 | tf_op jit(solution)/shard_map/reduce_scatter | solution.py:236
  697.4 21.7 %all-reduce.6.cloned.1.call-done = (bf16[128,192]{0,1:T(8,128)(2,1)}, bf16[192,128]{1,0:T(8,128)(2,1)}) async-done(((bf16[128,192]{0,1:T(8,128)(2,1)}, bf16[192,128]{1,0:T(8,128)(2,1)}), (bf16[128,192]{0,1:T(8,128)(2,1)}, bf16[192,128]{1,0:T(8,128)(2,1)})) %all-reduce.6.cloned.1.call-update) | async-done | bytes 98320 | tf_op jit(solution)/shard_map/psum | solution.py:229
  719.1 1.4 bitcast_convert_fusion.1
  721.2 1.4 bitcast_convert_fusion
  722.7 68.0 %all-reduce.4.cloned.1.call-done = f32[1,2,120,128]{3,2,1,0:T(8,128)} async-done(((f32[1,2,120,128]{3,2,1,0:T(8,128)}), f32[1,2,120,128]{3,2,1,0:T(8,128)}) %all-reduce.4.cloned.1.call-update) | async-done | bytes 122896 | tf_op jit(solution)/shard_map/psum | solution.py:227
  790.7 4.1 copy.115
  794.8 4.2 copy.116
  (559 shorter events, 166.0 us)
Async XLA Ops:
  8.0 447.8 %copy-start = (bf16[1,128,768]{2,1,0:T(8,128)(2,1)S(1)}, bf16[1,128,768]{2,1,0:T(8,128)(2,1)}, u32[]{:S(2)}) copy-start(bf16[1,128,768]{2,1,0:T(8,128)(2,1)} %param.12) | copy-start | bytes 589828
  8.6 5.3 copy-start.12
  8.7 5.3 copy-start.14
  22.9 7.1 copy-start.19
  22.9 249.0 %copy-start.16 = (f32[1,2,120,128]{3,2,1,0:T(8,128)S(1)}, f32[1,2,120,128]{3,2,1,0:T(8,128)}, u32[]{:S(2)}) copy-start(f32[1,2,120,128]{3,2,1,0:T(8,128)} %param.14) | copy-start | bytes 368644
  22.9 257.3 %all-to-all-start = ((bf16[2,60,2,120,128]{4,2,1,0,3:T(2,128)(2,1)}), bf16[2,60,2,120,128]{4,2,1,0,3:T(2,128)(2,1)}, u32[]{:S(2)}, u32[]{:S(2)}) async-start(bf16[2,60,2,120,128]{4,2,1,0,3:T(2,128)(2,1)} %copy.39), calls=%async_computation | async-start | bytes 14745600 | tf_op jit(solution)/shard_map/all_to_all | solution.py:98
  271.7 4.5 copy-start.5
  271.9 27.8 %copy-start.8 = (f32[120,128]{1,0:T(8,128)}, f32[120,128]{1,0:T(8,128)S(1)}, u32[]{:S(2)}) copy-start(f32[120,128]{1,0:T(8,128)S(1)} %get-tuple-element.233) | copy-start | bytes 184324
  271.9 27.8 %copy-start.10 = (f32[120,128]{1,0:T(8,128)}, f32[120,128]{1,0:T(8,128)S(1)}, u32[]{:S(2)}) copy-start(f32[120,128]{1,0:T(8,128)S(1)} %get-tuple-element.234) | copy-start | bytes 184324
  299.6 8.6 %copy-start.7 = (bf16[60,120,120,1,1]{2,0,1,4,3:T(8,128)(2,1)S(1)}, bf16[60,120,120,1,1]{2,0,1,4,3:T(8,128)(2,1)}, u32[]{:S(2)}) copy-start(bf16[60,120,120,1,1]{2,0,1,4,3:T(8,128)(2,1)} %get-tuple-element.231) | copy-start | bytes 5184004
  331.1 89.7 %all-to-all-start.1 = ((bf16[2,120,2,60,128]{4,2,0,3,1:T(2,128)(2,1)}), bf16[2,120,2,60,128]{4,2,0,3,1:T(2,128)(2,1)}, u32[]{:S(2)}, u32[]{:S(2)}) async-start(bf16[2,120,2,60,128]{4,2,0,3,1:T(2,128)(2,1)} %copy.45), calls=%async_computation.1 | async-start | bytes 14745600 | tf_op jit(solution)/shard_map/all_to_all | solution.py:102
  455.8 17.1 %copy-start.20 = (bf16[1,768,128]{2,1,0:T(8,128)(2,1)S(1)}, bf16[1,768,128]{2,1,0:T(8,128)(2,1)}, u32[]{:S(2)}) copy-start(bf16[1,768,128]{2,1,0:T(8,128)(2,1)} %param.13) | copy-start | bytes 589828
  472.9 30.9 %copy-start.2 = (bf16[14400,128]{1,0:T(8,128)(2,1)S(1)}, bf16[14400,128]{1,0:T(8,128)(2,1)}, u32[]{:S(2)}) copy-start(bf16[14400,128]{1,0:T(8,128)(2,1)} %bitcast_multiply_fusion) | copy-start | bytes 11059204
  514.8 3.0 copy-start.1
  522.4 47.1 %all-to-all-start.2 = ((bf16[60,2,120,128]{3,1,0,2:T(2,128)(2,1)}), bf16[60,2,120,128]{3,1,0,2:T(2,128)(2,1)}, u32[]{:S(2)}, u32[]{:S(2)}) async-start(bf16[60,2,120,128]{3,1,0,2:T(2,128)(2,1)} %copy.50), calls=%async_computation.2 | async-start | bytes 7372800 | tf_op jit(solution)/shard_map/all_to_all | solution.py:194
  527.8 16.7 %copy-start.18 = (f32[60]{0:T(128)S(1)}, f32[60]{0:T(128)}, u32[]{:S(2)}) copy-start(f32[60]{0:T(128)} %get-tuple-element.212) | copy-start | bytes 724
  550.1 24.1 %copy-start.4 = (bf16[60,120,120,1]{2,0,1,3:T(8,128)(2,1)S(1)}, bf16[60,120,120,1]{2,0,1,3:T(8,128)(2,1)}, u32[]{:S(2)}) copy-start(bf16[60,120,120,1]{2,0,1,3:T(8,128)(2,1)} %get-tuple-element.232) | copy-start | bytes 5184004
  550.1 172.6 %collective-permute-start = (bf16[1,1,60,240,128]{4,3,2,1,0:T(8,128)(2,1)}, bf16[1,1,60,240,128]{4,3,2,1,0:T(8,128)(2,1)}, u32[]{:S(2)}, u32[]{:S(2)}) collective-permute-start(bf16[1,1,60,240,128]{4,3,2,1,0:T(8,128)(2,1)} %multiply_convert_fusion.6), channel_id=1, source_target_pairs={{0,8},{8,16},{16,24},{1,9},{9,17},{17,25},{2,10},{10,18},{18,26},{... | collective-permute-start | bytes 11059208 | tf_op jit(solution)/shard_map/ppermute | solution.py:16
  569.5 6.7 slice-start
  574.2 2.2 slice-start.1
  574.2 2.2 copy-start.9
  574.2 2.2 copy-start.11
  576.4 2.3 copy-start.6
  588.3 46.3 %all-to-all-start.3 = ((bf16[120,2,60,128]{3,1,2,0:T(2,128)(2,1)}), bf16[120,2,60,128]{3,1,2,0:T(2,128)(2,1)}, u32[]{:S(2)}, u32[]{:S(2)}) async-start(bf16[120,2,60,128]{3,1,2,0:T(2,128)(2,1)} %copy.56), calls=%async_computation.3 | async-start | bytes 7372800 | tf_op jit(solution)/shard_map/all_to_all | solution.py:216
  593.7 81.2 %reduce-scatter.3.cloned.1.call-start = ((), (), s32[]{:S(2)}) async-start(), calls=%async_computation.7 | async-start | bytes 245760 | tf_op jit(solution)/shard_map/reduce_scatter | solution.py:233
  608.6 88.7 %reduce-scatter.5.cloned.1.call-start = ((), (), s32[]{:S(2)}) async-start(), calls=%async_computation.8 | async-start | bytes 245760 | tf_op jit(solution)/shard_map/reduce_scatter | solution.py:236
  639.6 6.6 copy-start.13
  639.6 6.6 copy-start.15
  646.2 8.7 %copy-start.3 = (bf16[14400,128]{1,0:T(8,128)(2,1)S(1)}, bf16[14400,128]{1,0:T(8,128)(2,1)}, u32[]{:S(2)}) copy-start(bf16[14400,128]{1,0:T(8,128)(2,1)} %bitcast_multiply_fusion) | copy-start | bytes 11059204
  653.6 69.1 %collective-permute-start.1 = (bf16[1,1,60,240,128]{4,3,2,1,0:T(8,128)(2,1)}, bf16[1,1,60,240,128]{4,3,2,1,0:T(8,128)(2,1)}, u32[]{:S(2)}, u32[]{:S(2)}) collective-permute-start(bf16[1,1,60,240,128]{4,3,2,1,0:T(8,128)(2,1)} %fusion.36), channel_id=1, source_target_pairs={{8,0},{16,8},{24,16},{9,1},{17,9},{25,17},{10,2},{18,10},{26,18},{... | collective-permute-start | bytes 11059208 | tf_op jit(solution)/shard_map/ppermute | solution.py:16
  674.9 44.2 %all-reduce.6.cloned.1.call-start = ((), (), s32[]{:S(2)}) async-start(), calls=%async_computation.9 | async-start | bytes 196608 | tf_op jit(solution)/shard_map/psum | solution.py:229
  697.3 93.4 %all-reduce.4.cloned.1.call-start = ((), (), s32[]{:S(2)}) async-start(), calls=%async_computation.6 | async-start | bytes 245760 | tf_op jit(solution)/shard_map/psum | solution.py:227
  794.8 4.2 copy-start.17
Sparse Core Ops, SparseCore 0:
  608.7 21.2 reduce-scatter.2
  675.0 22.2 reduce-scatter.4
  699.6 19.4 all-reduce.5
Sparse Core Ops, SparseCore 1:
  721.3 69.3 all-reduce.3
where the time goes:
time: 813 us; the launch traced here: 807 us
  waiting for transfers between devices  221 us (27%)
  matrix products  161 us (20%)
  local copies, waits for them, and re-layouts  153 us (19%)
  other arithmetic  146 us (18%)
  loops' own time  80.9 us (10%)
  starting transfers between devices  29.2 us (4%)
  between operations  15.8 us (2%)
    dynamic_update_slice x120, other arithmetic, legendre(): lax.scan(advance, (zero_rows, zero_rows), jnp.arange(cycles, dtype=jnp.in...  87.6 us
    another operation x1, loops' own time, legendre(): lax.scan(advance, (zero_rows, zero_rows), jnp.arange(cycles, dtype=jnp.in...  80.9 us
    dynamic_slice x120, local copies, waits for them, and re-layouts, legendre(): lax.scan(advance, (zero_rows, zero_rows), jnp.arange(cycles, dtype=jnp.in...  69.9 us
    psum x1, waiting for transfers between devices, on_device(): filter_grad = lax.psum(jnp.stack([filter_real, filter_imag]), ('sp', 'dp'))  68 us
    all_to_all x1, waiting for transfers between devices, joint_cycles(): return lax.all_to_all(values, 'sp', split_axis=1, concat_axis=3, tiled=True)  67 us
    dot_general x1, matrix products, backward_rows(): jnp.dot(masked, contract.T, preferred_element_type=jnp.float32)  30.9 us
    all_to_all x1, waiting for transfers between devices, on_device(): lax.all_to_all(grad_coeffs, 'sp', split_axis=0, concat_axis=2, tiled=True)  25.9 us
    reduce_scatter x1, waiting for transfers between devices, on_device(): lax.psum_scatter(summed[1].astype(jnp.bfloat16), 'dp', scatter_dimension=...  22.3 us
  transfers between devices with their start and end apart: 10, of which 6 were waited for; matrix products, arithmetic and copies ran while one was open for 35% of the time, Pallas kernels for 0%

commit v1 on v0

--- a/solution.py
+++ b/solution.py
@@ -8,6 +8,12 @@
 NLON = 240
 ROOT_HALF = 0.7071067811865476
 INV_ROOT_TAU = 0.3989422804014327
+
+
+def summed_here(x, axis):
+    parts = lax.all_gather(x, axis, axis=0, tiled=False)
+    total = parts.sum(axis=0)
+    return total
 
 
 def from_behind(block, axis, distance):
@@ -224,7 +230,7 @@
         (grad_mixed.reshape(grid_shape) + grad_tokens) * cycle_mask[:, None, None]
     ).astype(jnp.bfloat16)
     sent_back = from_behind(input_grad[None, None], "pipe", -1)
-    filter_grad = lax.psum(jnp.stack([filter_real, filter_imag]), ("sp", "dp"))
+    filter_grad = summed_here(jnp.stack([filter_real, filter_imag]), ("sp", "dp"))
     summed = (
         lax.psum(grad_expand.astype(jnp.bfloat16), "sp").astype(jnp.float32),
         lax.psum(grad_reduce.astype(jnp.bfloat16), "sp").astype(jnp.float32),

time: 813 us -> 777 us (0.956)
  waiting for transfers between devices: 221 us -> 153 us
  blocking collectives: 0 us -> 34.4 us
    psum x1 -> x0, waiting for transfers between devices: 68 us -> none  [on_device(): filter_grad = lax.psum(jnp.stack([filter_real, filter_imag]), ('sp', 'dp'))]
    all_gather x0 -> x1, blocking collectives: none -> 34.4 us  [summed_here(): parts = lax.all_gather(x, axis, axis=0, tiled=False)]
  transfers between devices with their start and end apart: 10 -> 9, of which waited for: 6 -> 5; matrix products, arithmetic and copies ran while one was open for 35% -> 37% of each run, Pallas kernels for 0% -> 0%
where the time goes in v1:
time: 777 us; the launch traced here: 771 us
  matrix products  161 us (21%)
  waiting for transfers between devices  153 us (20%)
  local copies, waits for them, and re-layouts  152 us (20%)
  other arithmetic  146 us (19%)
  loops' own time  80.9 us (10%)
  blocking collectives  34.4 us (4%)
  starting transfers between devices  29.1 us (4%)
  between operations  14.4 us (2%)
    dynamic_update_slice x120, other arithmetic, legendre(): lax.scan(advance, (zero_rows, zero_rows), jnp.arange(cycles, dtype=jnp.in...  87.6 us
    another operation x1, loops' own time, legendre(): lax.scan(advance, (zero_rows, zero_rows), jnp.arange(cycles, dtype=jnp.in...  80.9 us
    dynamic_slice x120, local copies, waits for them, and re-layouts, legendre(): lax.scan(advance, (zero_rows, zero_rows), jnp.arange(cycles, dtype=jnp.in...  69.9 us
    all_to_all x1, waiting for transfers between devices, joint_cycles(): return lax.all_to_all(values, 'sp', split_axis=1, concat_axis=3, tiled=True)  67 us
    all_gather x1, blocking collectives, summed_here(): parts = lax.all_gather(x, axis, axis=0, tiled=False)  34.4 us
    dot_general x1, matrix products, backward_rows(): jnp.dot(masked, contract.T, preferred_element_type=jnp.float32)  31 us
    all_to_all x1, waiting for transfers between devices, on_device(): lax.all_to_all(grad_coeffs, 'sp', split_axis=0, concat_axis=2, tiled=True)  25.9 us
    reduce_scatter x1, waiting for transfers between devices, on_device(): lax.psum_scatter(summed[1].astype(jnp.bfloat16), 'dp', scatter_dimension=...  22.3 us
  transfers between devices with their start and end apart: 9, of which 5 were waited for; matrix products, arithmetic and copies ran while one was open for 37% of the time, Pallas kernels for 0%

profile of v1, /device:TPU:0, one launch (start us, length us, event | category | flops | bytes accessed | tf_op | source)
XLA Modules:
  0.0 771.5 jit_solution(3760414547476445550)
XLA Ops:
  7.8 5.3 fusion.33
  13.2 8.8 %copy.39 = bf16[2,60,2,120,128]{4,2,1,0,3:T(2,128)(2,1)} copy(bf16[2,60,2,120,128]{4,3,2,1,0:T(8,128)(2,1)S(1)} %bitcast.168) | data formatting | bytes 14745600 | tf_op jit(solution)/shard_map/reshape | solution.py:117
  22.0 6.9 all-to-all-start
  29.2 240.9 %while.18 = (s32[]{:T(128)}, f32[60,120]{1,0:T(8,128)S(1)}, f32[60,120]{1,0:T(8,128)S(1)}, f32[120,60,120]{2,1,0:T(8,128)}, s32[120]{0:T(128)S(1)}, /*index=5*/f...) while((s32[]{:T(128)}, f32[60,120]{1,0:T(8,128)S(1)}, ...), condition=%wide.region_1.2_spmd.clone, body=%wide.region_0.1_spmd.clone.sunk | while | flops 65294 | bytes 151427 | solution.py:71
  271.1 4.3 broadcast_multiply_fusion
  275.5 3.9 fusion.61
  279.4 7.4 copy.41
  286.8 12.1 %convolution_bitcast_fusion = f32[2,60,2,120,128]{4,3,2,0,1:T(8,128)} fusion(bf16[2,120,2,60,128]{4,2,3,1,0:T(2,128)(2,1)} %bitcast.162, bf16[60,120,120,1,1]{2,0,1,4,3:T(8,128)(2,1)S(1)} %get-tuple-element.230), kind=kOutput, calls=%fused_computation.24 | convolution fusion | flops 884736000 | bytes 23846400 | tf_op jit(solution)/shard_map/tlj,sjrtc->strlc/dot_general | solution.py:119
  298.9 8.6 %subtract_convert_fusion = (bf16[2,60,1,120,128]{4,3,2,0,1:T(8,128)(2,1)}, bf16[2,60,1,120,128]{4,3,2,0,1:T(8,128)(2,1)}) fusion(f32[2,60,2,120,128]{4,3,2,0,1:T(8,128)} %convolution_bitcast_fusion, f32[120,128]{1,0:T(8,128)S(1)} %get-tuple-element.234, f32[120,128]{1,0:T(8,128)S(1)} %get-tuple-element.233), kind=kLoop, calls=%fused_computation.48 | loop fusion | flops 14745600 | bytes 22241280 | tf_op jit(solution)/shard_map/convert.6
  307.5 11.1 %convert_bitcast_fusion = bf16[2,120,2,60,128]{4,1,2,0,3:T(8,128)(2,1)} fusion(bf16[2,60,1,120,128]{4,3,2,0,1:T(8,128)(2,1)} %get-tuple-element.220, bf16[2,60,1,120,128]{4,3,2,0,1:T(8,128)(2,1)} %get-tuple-element.219, bf16[60,120,120,1,1]{2,0,1,4,3:T(8,128)(2,1)S(1)} %copy-done.7), kind=kOutput, calls=%fused_computation.46 | convolution fusion | flops 892108800 | bytes 16473600 | tf_op jit(solution)/shard_map/tlj,strlc->sjrtc/dot_general | solution.py:123
  318.5 11.9 %copy.45 = bf16[2,120,2,60,128]{4,2,0,3,1:T(2,128)(2,1)} copy(bf16[2,120,2,60,128]{4,1,2,0,3:T(8,128)(2,1)} %convert_bitcast_fusion) | data formatting | bytes 14745600 | tf_op jit(solution)/shard_map/convert_element_type | solution.py:125
  330.4 6.7 all-to-all-start.1
  337.1 9.4 %bitcast_multiply_fusion = bf16[14400,128]{1,0:T(8,128)(2,1)} fusion(bf16[1,1,60,240,128]{4,3,2,1,0:T(8,128)(2,1)} %param.11, bf16[14400]{0:T(1024)(128)(2,1)S(1)} %mul.489), kind=kLoop, calls=%fused_computation.58 | loop fusion | flops 1843200 | bytes 7401600 | tf_op jit(solution)/shard_map/mul | solution.py:144
  346.5 6.7 slice_bitcast_fusion
  353.1 67.0 %all-to-all-done.1 = bf16[2,120,2,60,128]{4,2,0,3,1:T(2,128)(2,1)} async-done(((bf16[2,120,2,60,128]{4,2,0,3,1:T(2,128)(2,1)}), bf16[2,120,2,60,128]{4,2,0,3,1:T(2,128)(2,1)}, u32[]{:S(2)}, u32[]{:S(2)}) %all-to-all-start.1) | async-done | bytes 7372832 | tf_op jit(solution)/shard_map/all_to_all | solution.py:108
  420.1 11.0 %copy.47 = bf16[2,60,2,2,60,128]{5,0,4,3,2,1:T(2,128)(2,1)S(1)} copy(bf16[2,60,2,2,60,128]{5,2,0,4,1,3:T(2,128)(2,1)} %bitcast.25) | data formatting | bytes 14745600 | tf_op jit(solution)/shard_map/all_to_all | solution.py:108
  431.1 7.3 fusion.30
  438.5 12.9 %fusion.100 = (f32[1,60,240,128]{3,2,1,0:T(8,128)S(1)}, bf16[1,60,240,128]{3,2,1,0:T(8,128)(2,1)}, bf16[1,60,240,128]{3,2,1,0:T(8,128)(2,1)S(1)}, f32[1,60,240,128]{3,2,1,0:T(8,128)}) fusion(f32[2,60,240,128]{3,2,1,0:T(8,128)} %fusion.30, bf16[1,1,60,240,128]{4,3,2,1,0:T(8,128)(2,1)} %param.9, bf16[1,1,60,240,128]{4,3,2,1,0:T(8,128)(2,1)} %param.10), kind=kLoop, calls=%fused_computation.174 | loop fusion | flops 11059200 | bytes 44236800 | tf_op jit(solution)/shard_map/slice | solution.py:184
  451.4 3.7 fusion.22
  455.1 17.1 %fusion.65 = f32[14400,768]{1,0:T(8,128)} fusion(bf16[14400,128]{1,0:T(8,128)(2,1)S(1)} %bitcast.163, bf16[1,128,768]{2,1,0:T(8,128)(2,1)S(1)} %copy-done), kind=kOutput, calls=%fused_computation.84 | convolution fusion | flops 2831155200 | bytes 48119808 | tf_op jit(solution)/shard_map/dot_general | solution.py:135
  472.1 31.0 %fusion.7 = bf16[14400,768]{1,0:T(8,128)(2,1)} fusion(f32[14400,768]{1,0:T(8,128)} %fusion.65, bf16[14400,128]{1,0:T(8,128)(2,1)} %bitcast.171, bf16[1,768,128]{2,1,0:T(8,128)(2,1)S(1)} %copy-done.19), kind=kOutput, calls=%fused_computation.14 | convolution fusion | flops 2941747200 | bytes 70238208 | tf_op jit(solution)/shard_map/dot_general | solution.py:146
  503.1 10.9 %convolution_add_fusion = f32[14400,128]{1,0:T(8,128)S(1)} fusion(bf16[14400,768]{1,0:T(8,128)(2,1)} %fusion.7, bf16[14400,128]{1,0:T(8,128)(2,1)S(1)} %copy-done.2, bf16[1,128,768]{2,1,0:T(8,128)(2,1)S(1)} %copy-done), kind=kOutput, calls=%fused_computation.22 | convolution fusion | flops 2834841600 | bytes 33374208 | tf_op jit(solution)/shard_map/dot_general | solution.py:149
  515.2 1.8 copy-done.1
  517.1 4.6 copy.50
  521.7 5.4 all-to-all-start.2
  527.1 16.7 %fusion.11 = f32[14400,128]{1,0:T(8,128)} fusion(bf16[14400,128]{1,0:T(8,128)(2,1)} %bitcast.174, f32[14400,128]{1,0:T(8,128)} %bitcast.167, bf16[14400,128]{1,0:T(8,128)(2,1)} %bitcast.173, bf16[1,768,128]{2,1,0:T(8,128)(2,1)S(1)} %copy-done.19, bf16[1,128,768]{2,1,0:T(8,128)(2,1)S(1)} %copy-done), kind=kOutput, calls=%fused_computation.21 | convolution fusion | flops 5723136000 | bytes 22511616 | tf_op jit(solution)/shard_map/dot_general | solution.py:137
  543.8 5.6 multiply_convert_fusion.6
  549.4 3.3 collective-permute-start
  552.6 16.1 %all-to-all-done.2 = bf16[60,2,120,128]{3,1,0,2:T(2,128)(2,1)} async-done(((bf16[60,2,120,128]{3,1,0,2:T(2,128)(2,1)}), bf16[60,2,120,128]{3,1,0,2:T(2,128)(2,1)}, u32[]{:S(2)}, u32[]{:S(2)}) %all-to-all-start.2) | async-done | bytes 3686432 | tf_op jit(solution)/shard_map/all_to_all | solution.py:200
  568.7 4.7 copy.52
  573.5 1.9 fusion.45
  575.7 2.3 add_reduce_fusion
  578.0 4.8 convert_bitcast_fusion.1
  582.7 4.8 copy.56
  587.6 5.4 all-to-all-start.3
  593.1 14.8 %convolution_convert_fusion = bf16[128,768]{0,1:T(8,128)(2,1)} fusion(bf16[14400,128]{1,0:T(8,128)(2,1)} %fusion.22, bf16[14400,768]{1,0:T(8,128)(2,1)} %fusion.7), kind=kOutput, calls=%fused_computation.76 | convolution fusion | flops 2831253504 | bytes 26001408 | tf_op jit(solution)/shard_map/dot_general | solution.py:148
  607.9 25.9 %all-to-all-done.3 = bf16[120,2,60,128]{3,1,2,0:T(2,128)(2,1)} async-done(((bf16[120,2,60,128]{3,1,2,0:T(2,128)(2,1)}), bf16[120,2,60,128]{3,1,2,0:T(2,128)(2,1)}, u32[]{:S(2)}, u32[]{:S(2)}) %all-to-all-start.3) | async-done | bytes 3686432 | tf_op jit(solution)/shard_map/all_to_all | solution.py:222
  633.8 5.1 copy.57
  638.9 6.6 reshape.336
  645.5 7.3 fusion.36
  654.2 20.1 %fusion.57 = bf16[768,128]{1,0:T(8,128)(2,1)} fusion(bf16[14400,128]{1,0:T(8,128)(2,1)S(1)} %copy-done.3, f32[14400,768]{1,0:T(8,128)} %fusion.65), kind=kOutput, calls=%fused_computation.75 | convolution fusion | flops 2886549504 | bytes 48119808 | tf_op jit(solution)/shard_map/dot_general | solution.py:145
  674.3 22.3 %reduce-scatter.5.cloned.1.call-done = bf16[192,128]{1,0:T(8,128)(2,1)} async-done(((bf16[768,128]{1,0:T(8,128)(2,1)}), bf16[192,128]{1,0:T(8,128)(2,1)}) %reduce-scatter.5.cloned.1.call-update) | async-done | bytes 49168 | tf_op jit(solution)/shard_map/reduce_scatter | solution.py:242
  696.7 21.8 %all-reduce.3.cloned.1.call-done = (bf16[128,192]{0,1:T(8,128)(2,1)}, bf16[192,128]{1,0:T(8,128)(2,1)}) async-done(((bf16[128,192]{0,1:T(8,128)(2,1)}, bf16[192,128]{1,0:T(8,128)(2,1)}), (bf16[128,192]{0,1:T(8,128)(2,1)}, bf16[192,128]{1,0:T(8,128)(2,1)})) %all-reduce.3.cloned.1.call-update) | async-done | bytes 98320 | tf_op jit(solution)/shard_map/psum | solution.py:235
  718.4 1.4 bitcast_convert_fusion.1
  719.9 1.4 bitcast_convert_fusion
  721.3 34.4 %all-gather = f32[16,120,128]{2,1,0:T(8,128)S(1)} all-gather(f32[2,120,128]{2,1,0:T(8,128)S(1)} %pad_maximum_fusion.2), channel_id=2, replica_groups=mesh['pipe'=4,'sp'=2,'dp'=4] {'sp','dp'}, dimensions={0}, use_global_device_ids=true | all-gather | bytes 1105920 | tf_op jit(solution)/shard_map/all_gather | solution.py:14
  756.4 4.1 copy.114
  760.6 4.1 copy.115
  (555 shorter events, 165.4 us)
Async XLA Ops:
  7.2 447.9 %copy-start = (bf16[1,128,768]{2,1,0:T(8,128)(2,1)S(1)}, bf16[1,128,768]{2,1,0:T(8,128)(2,1)}, u32[]{:S(2)}) copy-start(bf16[1,128,768]{2,1,0:T(8,128)(2,1)} %param.12) | copy-start | bytes 589828
  7.8 5.3 copy-start.12
  7.8 5.3 copy-start.14
  22.0 7.1 copy-start.18
  22.0 249.1 %copy-start.16 = (f32[1,2,120,128]{3,2,1,0:T(8,128)S(1)}, f32[1,2,120,128]{3,2,1,0:T(8,128)}, u32[]{:S(2)}) copy-start(f32[1,2,120,128]{3,2,1,0:T(8,128)} %param.14) | copy-start | bytes 368644
  22.0 257.4 %all-to-all-start = ((bf16[2,60,2,120,128]{4,2,1,0,3:T(2,128)(2,1)}), bf16[2,60,2,120,128]{4,2,1,0,3:T(2,128)(2,1)}, u32[]{:S(2)}, u32[]{:S(2)}) async-start(bf16[2,60,2,120,128]{4,2,1,0,3:T(2,128)(2,1)} %copy.39), calls=%async_computation | async-start | bytes 14745600 | tf_op jit(solution)/shard_map/all_to_all | solution.py:104
  271.0 4.5 copy-start.5
  271.1 27.8 %copy-start.8 = (f32[120,128]{1,0:T(8,128)}, f32[120,128]{1,0:T(8,128)S(1)}, u32[]{:S(2)}) copy-start(f32[120,128]{1,0:T(8,128)S(1)} %get-tuple-element.233) | copy-start | bytes 184324
  271.1 27.8 %copy-start.10 = (f32[120,128]{1,0:T(8,128)}, f32[120,128]{1,0:T(8,128)S(1)}, u32[]{:S(2)}) copy-start(f32[120,128]{1,0:T(8,128)S(1)} %get-tuple-element.234) | copy-start | bytes 184324
  298.9 8.6 %copy-start.7 = (bf16[60,120,120,1,1]{2,0,1,4,3:T(8,128)(2,1)S(1)}, bf16[60,120,120,1,1]{2,0,1,4,3:T(8,128)(2,1)}, u32[]{:S(2)}) copy-start(bf16[60,120,120,1,1]{2,0,1,4,3:T(8,128)(2,1)} %get-tuple-element.231) | copy-start | bytes 5184004
  330.4 89.7 %all-to-all-start.1 = ((bf16[2,120,2,60,128]{4,2,0,3,1:T(2,128)(2,1)}), bf16[2,120,2,60,128]{4,2,0,3,1:T(2,128)(2,1)}, u32[]{:S(2)}, u32[]{:S(2)}) async-start(bf16[2,120,2,60,128]{4,2,0,3,1:T(2,128)(2,1)} %copy.45), calls=%async_computation.1 | async-start | bytes 14745600 | tf_op jit(solution)/shard_map/all_to_all | solution.py:108
  455.1 17.1 %copy-start.19 = (bf16[1,768,128]{2,1,0:T(8,128)(2,1)S(1)}, bf16[1,768,128]{2,1,0:T(8,128)(2,1)}, u32[]{:S(2)}) copy-start(bf16[1,768,128]{2,1,0:T(8,128)(2,1)} %param.13) | copy-start | bytes 589828
  472.1 31.0 %copy-start.2 = (bf16[14400,128]{1,0:T(8,128)(2,1)S(1)}, bf16[14400,128]{1,0:T(8,128)(2,1)}, u32[]{:S(2)}) copy-start(bf16[14400,128]{1,0:T(8,128)(2,1)} %bitcast_multiply_fusion) | copy-start | bytes 11059204
  514.0 3.0 copy-start.1
  521.7 47.1 %all-to-all-start.2 = ((bf16[60,2,120,128]{3,1,0,2:T(2,128)(2,1)}), bf16[60,2,120,128]{3,1,0,2:T(2,128)(2,1)}, u32[]{:S(2)}, u32[]{:S(2)}) async-start(bf16[60,2,120,128]{3,1,0,2:T(2,128)(2,1)} %copy.50), calls=%async_computation.2 | async-start | bytes 7372800 | tf_op jit(solution)/shard_map/all_to_all | solution.py:200
  527.1 16.7 %copy-start.17 = (f32[60]{0:T(128)S(1)}, f32[60]{0:T(128)}, u32[]{:S(2)}) copy-start(f32[60]{0:T(128)} %get-tuple-element.212) | copy-start | bytes 724
  549.3 24.1 %copy-start.4 = (bf16[60,120,120,1]{2,0,1,3:T(8,128)(2,1)S(1)}, bf16[60,120,120,1]{2,0,1,3:T(8,128)(2,1)}, u32[]{:S(2)}) copy-start(bf16[60,120,120,1]{2,0,1,3:T(8,128)(2,1)} %get-tuple-element.232) | copy-start | bytes 5184004
  549.4 207.1 %collective-permute-start = (bf16[1,1,60,240,128]{4,3,2,1,0:T(8,128)(2,1)}, bf16[1,1,60,240,128]{4,3,2,1,0:T(8,128)(2,1)}, u32[]{:S(2)}, u32[]{:S(2)}) collective-permute-start(bf16[1,1,60,240,128]{4,3,2,1,0:T(8,128)(2,1)} %multiply_convert_fusion.6), channel_id=1, source_target_pairs={{0,8},{8,16},{16,24},{1,9},{9,17},{17,25},{2,10},{10,18},{18,26},{... | collective-permute-start | bytes 11059208 | tf_op jit(solution)/shard_map/ppermute | solution.py:22
  568.7 6.7 slice-start
  573.5 2.2 slice-start.1
  573.5 2.2 copy-start.9
  573.5 2.2 copy-start.11
  575.7 2.3 copy-start.6
  587.6 46.3 %all-to-all-start.3 = ((bf16[120,2,60,128]{3,1,2,0:T(2,128)(2,1)}), bf16[120,2,60,128]{3,1,2,0:T(2,128)(2,1)}, u32[]{:S(2)}, u32[]{:S(2)}) async-start(bf16[120,2,60,128]{3,1,2,0:T(2,128)(2,1)} %copy.56), calls=%async_computation.3 | async-start | bytes 7372800 | tf_op jit(solution)/shard_map/all_to_all | solution.py:222
  593.0 81.3 %reduce-scatter.3.cloned.1.call-start = ((), (), s32[]{:S(2)}) async-start(), calls=%async_computation.6 | async-start | bytes 245760 | tf_op jit(solution)/shard_map/reduce_scatter | solution.py:239
  607.9 88.8 %reduce-scatter.5.cloned.1.call-start = ((), (), s32[]{:S(2)}) async-start(), calls=%async_computation.7 | async-start | bytes 245760 | tf_op jit(solution)/shard_map/reduce_scatter | solution.py:242
  638.9 6.6 copy-start.13
  638.9 6.6 copy-start.15
  645.5 8.6 %copy-start.3 = (bf16[14400,128]{1,0:T(8,128)(2,1)S(1)}, bf16[14400,128]{1,0:T(8,128)(2,1)}, u32[]{:S(2)}) copy-start(bf16[14400,128]{1,0:T(8,128)(2,1)} %bitcast_multiply_fusion) | copy-start | bytes 11059204
  652.9 103.6 %collective-permute-start.1 = (bf16[1,1,60,240,128]{4,3,2,1,0:T(8,128)(2,1)}, bf16[1,1,60,240,128]{4,3,2,1,0:T(8,128)(2,1)}, u32[]{:S(2)}, u32[]{:S(2)}) collective-permute-start(bf16[1,1,60,240,128]{4,3,2,1,0:T(8,128)(2,1)} %fusion.36), channel_id=1, source_target_pairs={{8,0},{16,8},{24,16},{9,1},{17,9},{25,17},{10,2},{18,10},{26,18},{... | collective-permute-start | bytes 11059208 | tf_op jit(solution)/shard_map/ppermute | solution.py:22
  674.3 44.2 %all-reduce.3.cloned.1.call-start = ((), (), s32[]{:S(2)}) async-start(), calls=%async_computation.8 | async-start | bytes 196608 | tf_op jit(solution)/shard_map/psum | solution.py:235
Sparse Core Ops, SparseCore 0:
  608.0 21.2 reduce-scatter.2
  674.4 22.2 reduce-scatter.4
  699.0 19.4 all-reduce.2
